TPU v7x, 256 devices: a whole 4x4x8 slice. The times are simulated.
256 devices in a mesh: space: 16 (over z, core), tracer: 4 (over x), month: 4 (over y).
Axes of the slice: x: 4, y: 4, z: 8, core: 2. Of those that a mesh axis runs over, the one named last changes fastest.
Arguments:
- state: float32 [32, 16, 128, 512], P('tracer', 'month', 'space'), may hold values from -20 to 20
- coefficients: bfloat16 [4, 27, 16, 128, 512], P('month', None, None, 'space'), may hold values from 0 to 1, as said below
- rates: float32 [32], P('tracer'), may hold values from 0.05 to 0.5
- land_mask: int32 [128, 512], P('space'), may hold values 0 or 1
- wet_levels: int32 [128, 512], P('space'), may hold values from 1 to 16
- basis: float32 [4, 32, 16, 128, 512], P(None, 'tracer', 'month', 'space'), may hold values from -20 to 20
Outputs:
- residual: float32 [32, 16, 128, 512], P('tracer', 'month', 'space')
- next_basis: float32 [32, 16, 128, 512], P('tracer', 'month', 'space')
- krylov: float32 [6], replicated
Inputs may be any that keep to these rules, and one draw needn't show every extreme that they name: `coefficients`: the 27 weights of a cell in a month are non-negative and sum to one.
All inputs are finite; a program needn't handle non-finite values. No bound on the sum of `land_mask` on one device may be relied on, other than what follows from the above.
Results may differ from a plain program's by a relative error of at most 0.0011.
Values may be sent and summed in bfloat16 or wider, within the bound.
No kernel may reach another device: no remote copies, remote signals or barrier semaphores. Data moves between devices by JAX's collectives and lax.ppermute only.
A program may use at most 64 MiB of HBM per device.

v0:
```python
import jax
import jax.numpy as jnp
from jax import lax
from jax.sharding import PartitionSpec as P


def padded_2(x, sides, width):
    for axis, dim in sides:
        size, length = (lax.axis_size(axis), x.shape[dim])
        up = [(i, (i + 1) % size) for i in range(size - 1)]
        down = [(j, i) for i, j in up]
        last = lax.slice_in_dim(x, length - width, length, axis=dim)
        initial = lax.slice_in_dim(x, 0, width, axis=dim)
        before = lax.ppermute(last, axis, up)
        after = lax.ppermute(initial, axis, down)
        x = jnp.concatenate([before, x, after], axis=dim)
    return x


def apply_stencil(padded, weights, grid_shape):
    levels, columns, lat_rows = grid_shape
    summed = jnp.zeros(padded.shape[:-3] + grid_shape, jnp.float32)
    for depth_shift in range(3):
        for across in range(3):
            for along_shift in range(3):
                weight = weights[depth_shift * 9 + across * 3 + along_shift].astype(jnp.float32)
                summed = (
                    summed
                    + weight
                    * padded[
                        ...,
                        depth_shift : depth_shift + levels,
                        across : across + columns,
                        along_shift : along_shift + lat_rows,
                    ]
                )
    return summed


def on_device(state, coefficients, rates, land_mask, wet_levels, basis):
    tracers_here, levels_here, columns_here, rows_here = state.shape
    grid_shape = (levels_here, columns_here, rows_here)
    level_start = lax.axis_index("month") * levels_here
    level_index = level_start + jnp.arange(levels_here, dtype=jnp.int32)
    wet_cells = jnp.where(
        (land_mask[None] == 1) & (level_index[:, None, None] < wet_levels[None]), 1.0, 0.0
    ).astype(jnp.float32)
    uptake = rates[:, None, None, None]
    months_here = coefficients.shape[0]
    own_months = lax.all_to_all(coefficients, "month", split_axis=2, concat_axis=0, tiled=True)
    concentration = state * wet_cells
    tangent = basis[-1] * wet_cells
    for month_step in range(months_here * lax.axis_size("month")):
        weights = own_months[month_step]
        paired = jnp.stack([concentration, tangent])
        margins = padded_2(paired.astype(jnp.bfloat16), (("space", 3), ("month", 2)), 1).astype(
            paired.dtype
        )
        margins = jnp.pad(margins, ((0, 0), (0, 0), (0, 0), (0, 0), (1, 1)))
        transported = apply_stencil(margins, weights, grid_shape)
        square = concentration * concentration
        denominator = 1.0 + square
        new_concentration = wet_cells * (
            transported[0] - uptake * concentration * square / denominator
        )
        tangent = wet_cells * (
            transported[1]
            - uptake * square * (3.0 + square) / (denominator * denominator) * tangent
        )
        concentration = new_concentration
    residual = concentration - state
    jacobian_product = tangent - basis[-1]
    cell_count = float(
        state.size * lax.axis_size("space") * lax.axis_size("tracer") * lax.axis_size("month")
    )
    residual_squares = lax.psum(jnp.sum(residual * residual), ("space", "tracer", "month"))
    projected = (
        lax.psum(
            jnp.sum(basis * jacobian_product[None], axis=(1, 2, 3, 4)), ("space", "tracer", "month")
        )
        / cell_count
    )
    remainder = jacobian_product - jnp.sum(projected[:, None, None, None, None] * basis, axis=0)
    remainder_mean = (
        lax.psum(jnp.sum(remainder * remainder), ("space", "tracer", "month")) / cell_count
    )
    norm_scale = jnp.sqrt(remainder_mean + 1e-06)
    next_basis = remainder / norm_scale
    residual_rms = jnp.sqrt(residual_squares / cell_count + 1e-06)
    krylov = jnp.concatenate([projected, jnp.stack([norm_scale, residual_rms])])
    return (residual, next_basis, krylov)


def solution(mesh):
    return jax.shard_map(
        on_device,
        mesh=mesh,
        in_specs=(
            P("tracer", "month", "space", None),
            P("month", None, None, "space", None),
            P("tracer"),
            P("space", None),
            P("space", None),
            P(None, "tracer", "month", "space", None),
        ),
        out_specs=(P("tracer", "month", "space", None), P("tracer", "month", "space", None), P()),
        check_vma=False,
    )
```

profile of v0, /device:TPU:1, one launch (start us, length us, event | category | flops | bytes accessed | tf_op | source)
XLA Modules:
  0.0 331.2 jit_solution(2986459646332465918)
XLA Ops:
  0.6 4.1 %copy.10 = bf16[1,27,16,8,512]{4,3,1,0,2:T(8,128)(2,1)} copy(bf16[1,27,16,8,512]{4,3,2,1,0:T(8,128)(2,1)} %param.7) | data formatting | bytes 7077888 | tf_op args[1]
  4.7 5.1 %all-to-all-start = ((bf16[1,27,16,8,512]{4,3,1,0,2:T(8,128)(2,1)}), bf16[1,27,16,8,512]{4,3,1,0,2:T(8,128)(2,1)}, u32[]{:S(2)}, u32[]{:S(2)}) async-start(bf16[1,27,16,8,512]{4,3,1,0,2:T(8,128)(2,1)} %copy.10), calls=%async_computation | async-start | bytes 7077888 | tf_op jit(solution)/shard_map/all_to_all | solution.py:50
  9.9 0.1 and_select_fusion
  9.9 1.1 multiply_convert_fusion
  11.1 0.2 pad_maximum_fusion.23
  11.3 4.7 %collective-permute-start = (bf16[2,8,4,1,512]{4,3,2,1,0:T(2,128)(2,1)S(1)}, bf16[2,8,4,1,512]{4,3,2,1,0:T(2,128)(2,1)S(1)}, u32[]{:S(2)}, u32[]{:S(2)}) collective-permute-start(bf16[2,8,4,1,512]{4,3,2,1,0:T(2,128)(2,1)S(1)} %get-tuple-element.150), channel_id=1, source_target_pairs={{0,16},{16,32},{32,48},{48,64},{64,80},{80,96},{96,112},{112,128},... | collective-permute-start | bytes 196616 | tf_op jit(solution)/shard_map/ppermute | solution.py:14
  16.0 1.9 collective-permute-start.1
  17.9 4.7 %collective-permute-done.1 = bf16[2,8,4,1,512]{4,3,2,1,0:T(2,128)(2,1)S(1)} collective-permute-done((bf16[2,8,4,1,512]{4,3,2,1,0:T(2,128)(2,1)S(1)}, bf16[2,8,4,1,512]{4,3,2,1,0:T(2,128)(2,1)S(1)}, u32[]{:S(2)}, u32[]{:S(2)}) %collective-permute-start.1) | collective-permute-done | bytes 65568 | tf_op jit(solution)/shard_map/ppermute | solution.py:15
  22.7 0.3 pad_maximum_fusion.15
  23.0 3.6 %collective-permute-start.2 = (bf16[2,8,1,10,512]{4,3,2,1,0:T(8,128)(2,1)S(1)}, bf16[2,8,1,10,512]{4,3,2,1,0:T(8,128)(2,1)S(1)}, u32[]{:S(2)}, u32[]{:S(2)}) collective-permute-start(bf16[2,8,1,10,512]{4,3,2,1,0:T(8,128)(2,1)S(1)} %get-tuple-element.142), channel_id=1, source_target_pairs={{0,1},{1,2},{2,3},{4,5},{5,6},{6,7},{8,9},{9,10},{10,11},{12,13},{... | collective-permute-start | bytes 491528 | tf_op jit(solution)/shard_map/ppermute | solution.py:14
  26.6 1.3 collective-permute-start.3
  27.9 23.2 %collective-permute-done.2 = bf16[2,8,1,10,512]{4,3,2,1,0:T(8,128)(2,1)S(1)} collective-permute-done((bf16[2,8,1,10,512]{4,3,2,1,0:T(8,128)(2,1)S(1)}, bf16[2,8,1,10,512]{4,3,2,1,0:T(8,128)(2,1)S(1)}, u32[]{:S(2)}, u32[]{:S(2)}) %collective-permute-start.2) | collective-permute-done | bytes 163872 | tf_op jit(solution)/shard_map/ppermute | solution.py:14
  51.0 2.7 collective-permute-done.3
  53.7 0.7 maximum_convert_fusion
  54.5 1.8 fusion.300
  56.3 2.1 fusion.273
  58.3 8.0 %fusion.40 = f32[2,8,4,8,512]{4,3,2,1,0:T(8,128)} fusion(f32[2,8,6,10,512]{4,3,2,1,0:T(8,128)S(1)} %maximum_convert_fusion, f32[4,8,512]{2,1,0:T(8,128)} %get-tuple-element.102, f32[4,8,512]{2,1,0:T(8,128)} %get-tuple-element.103, f32[4,8,512]{2,1,0:T(8,128)} %get-tuple-element.104, f32[4,8,512]{2,1,0:T(8,128)} %get-tuple-element.105, ...), kind=kLoop, calls=%fused_computation.118 | loop fusion | flops 13893632 | bytes 15400960 | tf_op jit(solution)/shard_map/add | solution.py:28
  66.3 2.9 convert_bitcast_fusion.4
  69.2 0.2 pad_maximum_fusion.21
  69.4 6.9 %collective-permute-start.4 = (bf16[2,8,4,1,512]{4,3,2,1,0:T(2,128)(2,1)S(1)}, bf16[2,8,4,1,512]{4,3,2,1,0:T(2,128)(2,1)S(1)}, u32[]{:S(2)}, u32[]{:S(2)}) collective-permute-start(bf16[2,8,4,1,512]{4,3,2,1,0:T(2,128)(2,1)S(1)} %get-tuple-element.148), channel_id=1, source_target_pairs={{0,16},{16,32},{32,48},{48,64},{64,80},{80,96},{96,112},{112,128},... | collective-permute-start | bytes 196616 | tf_op jit(solution)/shard_map/ppermute | solution.py:14
  76.3 1.9 collective-permute-start.5
  78.2 2.1 fusion.301
  80.3 2.2 collective-permute-done.5
  82.6 0.3 pad_maximum_fusion.11
  82.9 3.1 collective-permute-start.6
  86.0 1.3 collective-permute-start.7
  87.3 2.0 fusion.302
  89.3 0.2 collective-permute-done.6
  89.5 4.1 %collective-permute-done.7 = bf16[2,8,1,10,512]{4,3,2,1,0:T(8,128)(2,1)S(1)} collective-permute-done((bf16[2,8,1,10,512]{4,3,2,1,0:T(8,128)(2,1)S(1)}, bf16[2,8,1,10,512]{4,3,2,1,0:T(8,128)(2,1)S(1)}, u32[]{:S(2)}, u32[]{:S(2)}) %collective-permute-start.7) | collective-permute-done | bytes 163872 | tf_op jit(solution)/shard_map/ppermute | solution.py:15
  93.6 0.7 maximum_convert_fusion.1
  94.3 8.0 %fusion.84 = f32[2,8,4,8,512]{4,3,2,1,0:T(8,128)} fusion(f32[2,8,6,10,512]{4,3,2,1,0:T(8,128)S(1)} %maximum_convert_fusion.1, f32[4,8,512]{2,1,0:T(8,128)} %get-tuple-element.75, f32[4,8,512]{2,1,0:T(8,128)} %get-tuple-element.76, f32[4,8,512]{2,1,0:T(8,128)} %get-tuple-element.77, f32[4,8,512]{2,1,0:T(8,128)} %get-tuple-element.79, ...), kind=kLoop, calls=%fused_computation.162 | loop fusion | flops 13893632 | bytes 15400960 | tf_op jit(solution)/shard_map/add | solution.py:28
  102.3 2.9 convert_bitcast_fusion.2
  105.2 0.2 pad_maximum_fusion.19
  105.4 4.6 %collective-permute-start.8 = (bf16[2,8,4,1,512]{4,3,2,1,0:T(2,128)(2,1)S(1)}, bf16[2,8,4,1,512]{4,3,2,1,0:T(2,128)(2,1)S(1)}, u32[]{:S(2)}, u32[]{:S(2)}) collective-permute-start(bf16[2,8,4,1,512]{4,3,2,1,0:T(2,128)(2,1)S(1)} %get-tuple-element.146), channel_id=1, source_target_pairs={{0,16},{16,32},{32,48},{48,64},{64,80},{80,96},{96,112},{112,128},... | collective-permute-start | bytes 196616 | tf_op jit(solution)/shard_map/ppermute | solution.py:14
  110.0 2.1 collective-permute-start.9
  112.1 4.2 %collective-permute-done.9 = bf16[2,8,4,1,512]{4,3,2,1,0:T(2,128)(2,1)S(1)} collective-permute-done((bf16[2,8,4,1,512]{4,3,2,1,0:T(2,128)(2,1)S(1)}, bf16[2,8,4,1,512]{4,3,2,1,0:T(2,128)(2,1)S(1)}, u32[]{:S(2)}, u32[]{:S(2)}) %collective-permute-start.9) | collective-permute-done | bytes 65568 | tf_op jit(solution)/shard_map/ppermute | solution.py:15
  116.3 0.3 pad_maximum_fusion.7
  116.6 2.9 collective-permute-start.10
  119.5 1.3 collective-permute-start.11
  120.8 2.1 fusion.221
  122.9 0.1 collective-permute-done.10
  123.0 4.1 %collective-permute-done.11 = bf16[2,8,1,10,512]{4,3,2,1,0:T(8,128)(2,1)S(1)} collective-permute-done((bf16[2,8,1,10,512]{4,3,2,1,0:T(8,128)(2,1)S(1)}, bf16[2,8,1,10,512]{4,3,2,1,0:T(8,128)(2,1)S(1)}, u32[]{:S(2)}, u32[]{:S(2)}) %collective-permute-start.11) | collective-permute-done | bytes 163872 | tf_op jit(solution)/shard_map/ppermute | solution.py:15
  127.1 0.7 maximum_convert_fusion.2
  127.8 8.0 %fusion.128 = f32[2,8,4,8,512]{4,3,2,1,0:T(8,128)} fusion(f32[2,8,6,10,512]{4,3,2,1,0:T(8,128)S(1)} %maximum_convert_fusion.2, f32[4,8,512]{2,1,0:T(8,128)} %get-tuple-element.48, f32[4,8,512]{2,1,0:T(8,128)} %get-tuple-element.49, f32[4,8,512]{2,1,0:T(8,128)} %get-tuple-element.50, f32[4,8,512]{2,1,0:T(8,128)} %get-tuple-element.51, ...), kind=kLoop, calls=%fused_computation.206 | loop fusion | flops 13893632 | bytes 15400960 | tf_op jit(solution)/shard_map/add | solution.py:28
  135.8 2.9 convert_bitcast_fusion
  138.7 0.2 pad_maximum_fusion.17
  138.8 4.6 %collective-permute-start.12 = (bf16[2,8,4,1,512]{4,3,2,1,0:T(2,128)(2,1)S(1)}, bf16[2,8,4,1,512]{4,3,2,1,0:T(2,128)(2,1)S(1)}, u32[]{:S(2)}, u32[]{:S(2)}) collective-permute-start(bf16[2,8,4,1,512]{4,3,2,1,0:T(2,128)(2,1)S(1)} %get-tuple-element.144), channel_id=1, source_target_pairs={{0,16},{16,32},{32,48},{48,64},{64,80},{80,96},{96,112},{112,128},... | collective-permute-start | bytes 196616 | tf_op jit(solution)/shard_map/ppermute | solution.py:14
  143.4 1.9 collective-permute-start.13
  145.4 4.3 %collective-permute-done.13 = bf16[2,8,4,1,512]{4,3,2,1,0:T(2,128)(2,1)S(1)} collective-permute-done((bf16[2,8,4,1,512]{4,3,2,1,0:T(2,128)(2,1)S(1)}, bf16[2,8,4,1,512]{4,3,2,1,0:T(2,128)(2,1)S(1)}, u32[]{:S(2)}, u32[]{:S(2)}) %collective-permute-start.13) | collective-permute-done | bytes 65568 | tf_op jit(solution)/shard_map/ppermute | solution.py:15
  149.7 0.3 pad_maximum_fusion.3
  150.0 2.4 collective-permute-start.14
  152.5 1.4 collective-permute-start.15
  153.9 2.1 fusion.303
  156.0 4.2 %collective-permute-done.15 = bf16[2,8,1,10,512]{4,3,2,1,0:T(8,128)(2,1)S(1)} collective-permute-done((bf16[2,8,1,10,512]{4,3,2,1,0:T(8,128)(2,1)S(1)}, bf16[2,8,1,10,512]{4,3,2,1,0:T(8,128)(2,1)S(1)}, u32[]{:S(2)}, u32[]{:S(2)}) %collective-permute-start.15) | collective-permute-done | bytes 163872 | tf_op jit(solution)/shard_map/ppermute | solution.py:15
  160.2 0.7 maximum_convert_fusion.3
  161.0 8.0 %fusion.172 = f32[2,8,4,8,512]{4,3,2,1,0:T(8,128)} fusion(f32[2,8,6,10,512]{4,3,2,1,0:T(8,128)S(1)} %maximum_convert_fusion.3, f32[4,8,512]{2,1,0:T(8,128)} %get-tuple-element.22, f32[4,8,512]{2,1,0:T(8,128)} %get-tuple-element.23, f32[4,8,512]{2,1,0:T(8,128)} %get-tuple-element.24, f32[4,8,512]{2,1,0:T(8,128)} %get-tuple-element.25, ...), kind=kLoop, calls=%fused_computation.250 | loop fusion | flops 13893632 | bytes 15400960 | tf_op jit(solution)/shard_map/add | solution.py:28
  169.0 3.8 %multiply_reduce_fusion.2 = (f32[]{:T(128)}, f32[8,4,8,512]{3,2,1,0:T(8,128)}, f32[8,4,8,512]{3,2,1,0:T(8,128)S(1)}) fusion(f32[8,4,8,512]{3,2,1,0:T(8,128)} %param.6, f32[8,4,8,512]{3,2,1,0:T(8,128)} %get-tuple-element.131, f32[8]{0:T(128)S(1)} %copy-done.9, f32[2,8,4,8,512]{4,3,2,1,0:T(8,128)} %fusion.172, f32[4,8,512]{2,1,0:T(8,128)S(1)} %and_select_fusion, ...), kind=kLoop, calls=%fused_computation.318 | loop fusion | flops 2490367 | bytes 4259876 | tf_op jit(solution)/shard_map/reduce_sum | solution.py:76
  172.8 0.3 multiply_reduce_fusion.1
  173.2 80.0 %psum.21 = f32[4]{0:T(128)S(1)} all-reduce(f32[4]{0:T(128)S(1)} %multiply_reduce_fusion.1), channel_id=1, replica_groups=mesh['space'=16,'tracer'=4,'month'=4] {'space','tracer','month'}, use_global_device_ids=true, to_apply=%region_1.2 | all-reduce | flops 4 | bytes 32 | tf_op jit(solution)/shard_map/psum | solution.py:78
  253.1 0.3 multiply_reduce_fusion
  253.5 0.8 multiply_reduce_fusion.3
  254.2 74.1 %all-reduce.4 = (f32[]{:T(128)}, f32[]{:T(128)}) all-reduce(f32[]{:T(128)} %get-tuple-element.7, f32[]{:T(128)} %get-tuple-element.5), channel_id=1, replica_groups=mesh['space'=16,'tracer'=4,'month'=4] {'space','tracer','month'}, use_global_device_ids=true, to_apply=%region_4.5 | all-reduce | flops 2 | bytes 16 | tf_op jit(solution)/shard_map/psum | solution.py:85
  329.7 0.9 broadcast_divide_fusion
  330.6 0.6 pad_maximum_fusion.24
  (30 shorter events, 0.1 us)
Async XLA Ops:
  4.7 5.1 %copy-start.7 = (s32[8,512]{1,0:T(8,128)S(1)}, s32[8,512]{1,0:T(8,128)}, u32[]{:S(2)}) copy-start(s32[8,512]{1,0:T(8,128)} %param.9) | copy-start | bytes 49156
  4.7 5.2 %copy-start.8 = (s32[8,512]{1,0:T(8,128)S(1)}, s32[8,512]{1,0:T(8,128)}, u32[]{:S(2)}) copy-start(s32[8,512]{1,0:T(8,128)} %param.10) | copy-start | bytes 49156
  4.7 6.4 %copy-start.1 = (f32[8,4,8,512]{3,2,1,0:T(8,128)S(1)}, f32[8,4,8,512]{3,2,1,0:T(8,128)}, u32[]{:S(2)}) copy-start(f32[8,4,8,512]{3,2,1,0:T(8,128)} %param.6) | copy-start | bytes 1572868
  4.7 49.8 %all-to-all-start = ((bf16[1,27,16,8,512]{4,3,1,0,2:T(8,128)(2,1)}), bf16[1,27,16,8,512]{4,3,1,0,2:T(8,128)(2,1)}, u32[]{:S(2)}, u32[]{:S(2)}) async-start(bf16[1,27,16,8,512]{4,3,1,0,2:T(8,128)(2,1)} %copy.10), calls=%async_computation | async-start | bytes 7077888 | tf_op jit(solution)/shard_map/all_to_all | solution.py:50
  11.3 6.6 %collective-permute-start = (bf16[2,8,4,1,512]{4,3,2,1,0:T(2,128)(2,1)S(1)}, bf16[2,8,4,1,512]{4,3,2,1,0:T(2,128)(2,1)S(1)}, u32[]{:S(2)}, u32[]{:S(2)}) collective-permute-start(bf16[2,8,4,1,512]{4,3,2,1,0:T(2,128)(2,1)S(1)} %get-tuple-element.150), channel_id=1, source_target_pairs={{0,16},{16,32},{32,48},{48,64},{64,80},{80,96},{96,112},{112,128},... | collective-permute-start | bytes 196616 | tf_op jit(solution)/shard_map/ppermute | solution.py:14
  16.0 6.7 %collective-permute-start.1 = (bf16[2,8,4,1,512]{4,3,2,1,0:T(2,128)(2,1)S(1)}, bf16[2,8,4,1,512]{4,3,2,1,0:T(2,128)(2,1)S(1)}, u32[]{:S(2)}, u32[]{:S(2)}) collective-permute-start(bf16[2,8,4,1,512]{4,3,2,1,0:T(2,128)(2,1)S(1)} %get-tuple-element.151), channel_id=1, source_target_pairs={{16,0},{32,16},{48,32},{64,48},{80,64},{96,80},{112,96},{128,112},... | collective-permute-start | bytes 196616 | tf_op jit(solution)/shard_map/ppermute | solution.py:15
  23.0 28.1 %collective-permute-start.2 = (bf16[2,8,1,10,512]{4,3,2,1,0:T(8,128)(2,1)S(1)}, bf16[2,8,1,10,512]{4,3,2,1,0:T(8,128)(2,1)S(1)}, u32[]{:S(2)}, u32[]{:S(2)}) collective-permute-start(bf16[2,8,1,10,512]{4,3,2,1,0:T(8,128)(2,1)S(1)} %get-tuple-element.142), channel_id=1, source_target_pairs={{0,1},{1,2},{2,3},{4,5},{5,6},{6,7},{8,9},{9,10},{10,11},{12,13},{... | collective-permute-start | bytes 491528 | tf_op jit(solution)/shard_map/ppermute | solution.py:14
  26.6 27.2 %collective-permute-start.3 = (bf16[2,8,1,10,512]{4,3,2,1,0:T(8,128)(2,1)S(1)}, bf16[2,8,1,10,512]{4,3,2,1,0:T(8,128)(2,1)S(1)}, u32[]{:S(2)}, u32[]{:S(2)}) collective-permute-start(bf16[2,8,1,10,512]{4,3,2,1,0:T(8,128)(2,1)S(1)} %get-tuple-element.143), channel_id=1, source_target_pairs={{1,0},{2,1},{3,2},{5,4},{6,5},{7,6},{9,8},{10,9},{11,10},{13,12},{... | collective-permute-start | bytes 491528 | tf_op jit(solution)/shard_map/ppermute | solution.py:15
  58.3 8.0 %copy-start.9 = (f32[8]{0:T(128)S(1)}, f32[8]{0:T(128)}, u32[]{:S(2)}) copy-start(f32[8]{0:T(128)} %param.8) | copy-start | bytes 100
  69.4 11.0 %collective-permute-start.4 = (bf16[2,8,4,1,512]{4,3,2,1,0:T(2,128)(2,1)S(1)}, bf16[2,8,4,1,512]{4,3,2,1,0:T(2,128)(2,1)S(1)}, u32[]{:S(2)}, u32[]{:S(2)}) collective-permute-start(bf16[2,8,4,1,512]{4,3,2,1,0:T(2,128)(2,1)S(1)} %get-tuple-element.148), channel_id=1, source_target_pairs={{0,16},{16,32},{32,48},{48,64},{64,80},{80,96},{96,112},{112,128},... | collective-permute-start | bytes 196616 | tf_op jit(solution)/shard_map/ppermute | solution.py:14
  76.3 6.3 %collective-permute-start.5 = (bf16[2,8,4,1,512]{4,3,2,1,0:T(2,128)(2,1)S(1)}, bf16[2,8,4,1,512]{4,3,2,1,0:T(2,128)(2,1)S(1)}, u32[]{:S(2)}, u32[]{:S(2)}) collective-permute-start(bf16[2,8,4,1,512]{4,3,2,1,0:T(2,128)(2,1)S(1)} %get-tuple-element.149), channel_id=1, source_target_pairs={{16,0},{32,16},{48,32},{64,48},{80,64},{96,80},{112,96},{128,112},... | collective-permute-start | bytes 196616 | tf_op jit(solution)/shard_map/ppermute | solution.py:15
  82.9 6.6 %collective-permute-start.6 = (bf16[2,8,1,10,512]{4,3,2,1,0:T(8,128)(2,1)S(1)}, bf16[2,8,1,10,512]{4,3,2,1,0:T(8,128)(2,1)S(1)}, u32[]{:S(2)}, u32[]{:S(2)}) collective-permute-start(bf16[2,8,1,10,512]{4,3,2,1,0:T(8,128)(2,1)S(1)} %get-tuple-element.140), channel_id=1, source_target_pairs={{0,1},{1,2},{2,3},{4,5},{5,6},{6,7},{8,9},{9,10},{10,11},{12,13},{... | collective-permute-start | bytes 491528 | tf_op jit(solution)/shard_map/ppermute | solution.py:14
  86.0 7.6 %collective-permute-start.7 = (bf16[2,8,1,10,512]{4,3,2,1,0:T(8,128)(2,1)S(1)}, bf16[2,8,1,10,512]{4,3,2,1,0:T(8,128)(2,1)S(1)}, u32[]{:S(2)}, u32[]{:S(2)}) collective-permute-start(bf16[2,8,1,10,512]{4,3,2,1,0:T(8,128)(2,1)S(1)} %get-tuple-element.141), channel_id=1, source_target_pairs={{1,0},{2,1},{3,2},{5,4},{6,5},{7,6},{9,8},{10,9},{11,10},{13,12},{... | collective-permute-start | bytes 491528 | tf_op jit(solution)/shard_map/ppermute | solution.py:15
  105.4 6.7 %collective-permute-start.8 = (bf16[2,8,4,1,512]{4,3,2,1,0:T(2,128)(2,1)S(1)}, bf16[2,8,4,1,512]{4,3,2,1,0:T(2,128)(2,1)S(1)}, u32[]{:S(2)}, u32[]{:S(2)}) collective-permute-start(bf16[2,8,4,1,512]{4,3,2,1,0:T(2,128)(2,1)S(1)} %get-tuple-element.146), channel_id=1, source_target_pairs={{0,16},{16,32},{32,48},{48,64},{64,80},{80,96},{96,112},{112,128},... | collective-permute-start | bytes 196616 | tf_op jit(solution)/shard_map/ppermute | solution.py:14
  110.0 6.3 %collective-permute-start.9 = (bf16[2,8,4,1,512]{4,3,2,1,0:T(2,128)(2,1)S(1)}, bf16[2,8,4,1,512]{4,3,2,1,0:T(2,128)(2,1)S(1)}, u32[]{:S(2)}, u32[]{:S(2)}) collective-permute-start(bf16[2,8,4,1,512]{4,3,2,1,0:T(2,128)(2,1)S(1)} %get-tuple-element.147), channel_id=1, source_target_pairs={{16,0},{32,16},{48,32},{64,48},{80,64},{96,80},{112,96},{128,112},... | collective-permute-start | bytes 196616 | tf_op jit(solution)/shard_map/ppermute | solution.py:15
  116.6 6.4 %collective-permute-start.10 = (bf16[2,8,1,10,512]{4,3,2,1,0:T(8,128)(2,1)S(1)}, bf16[2,8,1,10,512]{4,3,2,1,0:T(8,128)(2,1)S(1)}, u32[]{:S(2)}, u32[]{:S(2)}) collective-permute-start(bf16[2,8,1,10,512]{4,3,2,1,0:T(8,128)(2,1)S(1)} %get-tuple-element.138), channel_id=1, source_target_pairs={{0,1},{1,2},{2,3},{4,5},{5,6},{6,7},{8,9},{9,10},{10,11},{12,13},{... | collective-permute-start | bytes 491528 | tf_op jit(solution)/shard_map/ppermute | solution.py:14
  119.5 7.6 %collective-permute-start.11 = (bf16[2,8,1,10,512]{4,3,2,1,0:T(8,128)(2,1)S(1)}, bf16[2,8,1,10,512]{4,3,2,1,0:T(8,128)(2,1)S(1)}, u32[]{:S(2)}, u32[]{:S(2)}) collective-permute-start(bf16[2,8,1,10,512]{4,3,2,1,0:T(8,128)(2,1)S(1)} %get-tuple-element.139), channel_id=1, source_target_pairs={{1,0},{2,1},{3,2},{5,4},{6,5},{7,6},{9,8},{10,9},{11,10},{13,12},{... | collective-permute-start | bytes 491528 | tf_op jit(solution)/shard_map/ppermute | solution.py:15
  138.8 6.5 %collective-permute-start.12 = (bf16[2,8,4,1,512]{4,3,2,1,0:T(2,128)(2,1)S(1)}, bf16[2,8,4,1,512]{4,3,2,1,0:T(2,128)(2,1)S(1)}, u32[]{:S(2)}, u32[]{:S(2)}) collective-permute-start(bf16[2,8,4,1,512]{4,3,2,1,0:T(2,128)(2,1)S(1)} %get-tuple-element.144), channel_id=1, source_target_pairs={{0,16},{16,32},{32,48},{48,64},{64,80},{80,96},{96,112},{112,128},... | collective-permute-start | bytes 196616 | tf_op jit(solution)/shard_map/ppermute | solution.py:14
  143.4 6.3 %collective-permute-start.13 = (bf16[2,8,4,1,512]{4,3,2,1,0:T(2,128)(2,1)S(1)}, bf16[2,8,4,1,512]{4,3,2,1,0:T(2,128)(2,1)S(1)}, u32[]{:S(2)}, u32[]{:S(2)}) collective-permute-start(bf16[2,8,4,1,512]{4,3,2,1,0:T(2,128)(2,1)S(1)} %get-tuple-element.145), channel_id=1, source_target_pairs={{16,0},{32,16},{48,32},{64,48},{80,64},{96,80},{112,96},{128,112},... | collective-permute-start | bytes 196616 | tf_op jit(solution)/shard_map/ppermute | solution.py:15
  150.0 6.0 %collective-permute-start.14 = (bf16[2,8,1,10,512]{4,3,2,1,0:T(8,128)(2,1)S(1)}, bf16[2,8,1,10,512]{4,3,2,1,0:T(8,128)(2,1)S(1)}, u32[]{:S(2)}, u32[]{:S(2)}) collective-permute-start(bf16[2,8,1,10,512]{4,3,2,1,0:T(8,128)(2,1)S(1)} %get-tuple-element.136), channel_id=1, source_target_pairs={{0,1},{1,2},{2,3},{4,5},{5,6},{6,7},{8,9},{9,10},{10,11},{12,13},{... | collective-permute-start | bytes 491528 | tf_op jit(solution)/shard_map/ppermute | solution.py:14
  152.4 8.5 %copy-start.2 = (f32[4,8,512]{2,1,0:T(8,128)S(1)}, f32[4,8,512]{2,1,0:T(8,128)}, u32[]{:S(2)}) copy-start(f32[4,8,512]{2,1,0:T(8,128)} %get-tuple-element.40) | copy-start | bytes 196612
  152.4 8.5 %copy-start.3 = (f32[4,8,512]{2,1,0:T(8,128)S(1)}, f32[4,8,512]{2,1,0:T(8,128)}, u32[]{:S(2)}) copy-start(f32[4,8,512]{2,1,0:T(8,128)} %get-tuple-element.41) | copy-start | bytes 196612
  152.4 8.5 %copy-start.4 = (f32[4,8,512]{2,1,0:T(8,128)S(1)}, f32[4,8,512]{2,1,0:T(8,128)}, u32[]{:S(2)}) copy-start(f32[4,8,512]{2,1,0:T(8,128)} %get-tuple-element.42) | copy-start | bytes 196612
  152.5 8.5 %copy-start.5 = (f32[4,8,512]{2,1,0:T(8,128)S(1)}, f32[4,8,512]{2,1,0:T(8,128)}, u32[]{:S(2)}) copy-start(f32[4,8,512]{2,1,0:T(8,128)} %get-tuple-element.43) | copy-start | bytes 196612
  152.5 8.5 %copy-start.6 = (f32[4,8,512]{2,1,0:T(8,128)S(1)}, f32[4,8,512]{2,1,0:T(8,128)}, u32[]{:S(2)}) copy-start(f32[4,8,512]{2,1,0:T(8,128)} %get-tuple-element.44) | copy-start | bytes 196612
  152.5 7.8 %collective-permute-start.15 = (bf16[2,8,1,10,512]{4,3,2,1,0:T(8,128)(2,1)S(1)}, bf16[2,8,1,10,512]{4,3,2,1,0:T(8,128)(2,1)S(1)}, u32[]{:S(2)}, u32[]{:S(2)}) collective-permute-start(bf16[2,8,1,10,512]{4,3,2,1,0:T(8,128)(2,1)S(1)} %get-tuple-element.137), channel_id=1, source_target_pairs={{1,0},{2,1},{3,2},{5,4},{6,5},{7,6},{9,8},{10,9},{11,10},{13,12},{... | collective-permute-start | bytes 491528 | tf_op jit(solution)/shard_map/ppermute | solution.py:15
  169.0 3.8 %copy-start = (f32[4,8,4,8,512]{4,3,2,1,0:T(8,128)S(1)}, f32[4,8,4,8,512]{4,3,2,1,0:T(8,128)}, u32[]{:S(2)}) copy-start(f32[4,8,4,8,512]{4,3,2,1,0:T(8,128)} %param.11) | copy-start | bytes 6291460
where the time goes:
time: 333 us; the launch traced here: 331 us
  blocking collectives  154 us (46%)
  other arithmetic  65.5 us (20%)
  waiting for transfers between devices  54.1 us (16%)
  starting transfers between devices  51 us (15%)
  local copies, waits for them, and re-layouts  4.1 us (1%)
    psum x1, blocking collectives, on_device(): lax.psum(jnp.sum(basis * jacobian_product[None], axis=(1, 2, 3, 4)), ('sp...  80 us
    psum x1, blocking collectives, on_device(): lax.psum(jnp.sum(remainder * remainder), ('space', 'tracer', 'month'))  74.1 us
    ppermute x8, starting transfers between devices, padded_2(): before = lax.ppermute(last, axis, up)  32.7 us
    add x4, other arithmetic, apply_stencil(): summed + weight * padded[..., depth_shift:depth_shift + levels, across:ac...  31.9 us
    ppermute x8, waiting for transfers between devices, padded_2(): after = lax.ppermute(initial, axis, down)  30.6 us
    ppermute x8, waiting for transfers between devices, padded_2(): before = lax.ppermute(last, axis, up)  23.5 us
    ppermute x8, starting transfers between devices, padded_2(): after = lax.ppermute(initial, axis, down)  13.2 us
    convert_element_type x6, other arithmetic, apply_stencil(): weights[depth_shift * 9 + across * 3 + along_shift].astype(jnp.float32)  12.3 us
  transfers between devices with their start and end apart: 17, of which 11 were waited for; matrix products, arithmetic and copies ran while one was open for 3% of the time, Pallas kernels for 0%

commit v1 on v0

--- a/solution.py
+++ b/solution.py
@@ -37,6 +37,18 @@
     return summed
 
 
+def spread_sum(values, axes):
+    count = lax.axis_size(axes)
+    rows = jnp.broadcast_to(values[None], (count,) + values.shape)
+    return jnp.sum(lax.all_to_all(rows, axes, 0, 0, tiled=True), axis=0)
+
+
+def sum_everywhere(values):
+    row = jnp.zeros((1, 128), jnp.float32).at[0, : values.shape[0]].set(values)
+    row = spread_sum(row, ("tracer", "month"))
+    return spread_sum(row, ("space",))[0, : values.shape[0]]
+
+
 def on_device(state, coefficients, rates, land_mask, wet_levels, basis):
     tracers_here, levels_here, columns_here, rows_here = state.shape
     grid_shape = (levels_here, columns_here, rows_here)
@@ -73,20 +85,27 @@
     cell_count = float(
         state.size * lax.axis_size("space") * lax.axis_size("tracer") * lax.axis_size("month")
     )
-    residual_squares = lax.psum(jnp.sum(residual * residual), ("space", "tracer", "month"))
-    projected = (
-        lax.psum(
-            jnp.sum(basis * jacobian_product[None], axis=(1, 2, 3, 4)), ("space", "tracer", "month")
-        )
-        / cell_count
-    )
+    pairs = [(k, m) for k in range(4) for m in range(k, 4)]
+    parts = [jnp.sum(basis[k] * jacobian_product) for k in range(4)]
+    parts += [jnp.sum(jacobian_product * jacobian_product), jnp.sum(residual * residual)]
+    parts += [jnp.sum(basis[k] * basis[m]) for k, m in pairs]
+    means = sum_everywhere(jnp.stack(parts)) / cell_count
+    projected = means[:4]
+    gram_term = jnp.float32(0.0)
+    for place, (k, m) in enumerate(pairs):
+        gram_term += (1.0 if k == m else 2.0) * projected[k] * projected[m] * means[6 + place]
+    cross = 2.0 * jnp.sum(projected * projected)
     remainder = jacobian_product - jnp.sum(projected[:, None, None, None, None] * basis, axis=0)
-    remainder_mean = (
-        lax.psum(jnp.sum(remainder * remainder), ("space", "tracer", "month")) / cell_count
+    expanded = means[4] - cross + gram_term
+    remainder_mean = lax.cond(
+        expanded > 0.01 * (means[4] + cross + gram_term),
+        lambda r: expanded,
+        lambda r: sum_everywhere(jnp.sum(r * r)[None])[0] / cell_count,
+        remainder,
     )
     norm_scale = jnp.sqrt(remainder_mean + 1e-06)
     next_basis = remainder / norm_scale
-    residual_rms = jnp.sqrt(residual_squares / cell_count + 1e-06)
+    residual_rms = jnp.sqrt(means[5] + 1e-06)
     krylov = jnp.concatenate([projected, jnp.stack([norm_scale, residual_rms])])
     return (residual, next_basis, krylov)
 

time: 333 us -> 241 us (0.72)
  blocking collectives: 154 us -> 31 us
  between operations: 2.45 us -> 20.8 us
  local copies, waits for them, and re-layouts: 4.1 us -> 14.9 us
    psum x2 -> x0, blocking collectives: 154 us -> none  [the longest x1 80 us: on_device(): lax.psum(jnp.sum(basis * jacobian_product[None], axis=(1, 2, 3, 4)), ('sp...]
    all_to_all x0 -> x2, blocking collectives: none -> 31 us  [spread_sum(): return jnp.sum(lax.all_to_all(rows, axes, 0, 0, tiled=True), axis=0)]
    another operation x0 -> x1, local copies, waits for them, and re-layouts: none -> 10 us  [on_device(): means = sum_everywhere(jnp.stack(parts)) / cell_count]
  transfers between devices with their start and end apart: 17 -> 17, of which waited for: 11 -> 11; matrix products, arithmetic and copies ran while one was open for 3% -> 5% of each run, Pallas kernels for 0% -> 0%
where the time goes in v1:
time: 241 us; the launch traced here: 238 us
  other arithmetic  67.3 us (28%)
  waiting for transfers between devices  53.4 us (22%)
  starting transfers between devices  51 us (21%)
  blocking collectives  31 us (13%)
  between operations  20.8 us (9%)
  local copies, waits for them, and re-layouts  14.9 us (6%)
    ppermute x8, starting transfers between devices, padded_2(): before = lax.ppermute(last, axis, up)  32.7 us
    add x4, other arithmetic, apply_stencil(): summed + weight * padded[..., depth_shift:depth_shift + levels, across:ac...  31.8 us
    all_to_all x2, blocking collectives, spread_sum(): return jnp.sum(lax.all_to_all(rows, axes, 0, 0, tiled=True), axis=0)  31 us
    ppermute x8, waiting for transfers between devices, padded_2(): after = lax.ppermute(initial, axis, down)  29.9 us
    ppermute x8, waiting for transfers between devices, padded_2(): before = lax.ppermute(last, axis, up)  23.5 us
    ppermute x8, starting transfers between devices, padded_2(): after = lax.ppermute(initial, axis, down)  13.2 us
    convert_element_type x6, other arithmetic, apply_stencil(): weights[depth_shift * 9 + across * 3 + along_shift].astype(jnp.float32)  12.3 us
    another operation x1, local copies, waits for them, and re-layouts, on_device(): means = sum_everywhere(jnp.stack(parts)) / cell_count  10 us
  transfers between devices with their start and end apart: 17, of which 11 were waited for; matrix products, arithmetic and copies ran while one was open for 5% of the time, Pallas kernels for 0%

profile of v1, /device:TPU:1, one launch (start us, length us, event | category | flops | bytes accessed | tf_op | source)
XLA Modules:
  0.0 238.4 jit_solution(4976762386968576325)
XLA Ops:
  0.6 4.1 %copy.14 = bf16[1,27,16,8,512]{4,3,1,0,2:T(8,128)(2,1)} copy(bf16[1,27,16,8,512]{4,3,2,1,0:T(8,128)(2,1)} %param.13) | data formatting | bytes 7077888 | tf_op args[1]
  4.7 5.1 %all-to-all-start.2 = ((bf16[1,27,16,8,512]{4,3,1,0,2:T(8,128)(2,1)}), bf16[1,27,16,8,512]{4,3,1,0,2:T(8,128)(2,1)}, u32[]{:S(2)}, u32[]{:S(2)}) async-start(bf16[1,27,16,8,512]{4,3,1,0,2:T(8,128)(2,1)} %copy.14), calls=%async_computation.2 | async-start | bytes 7077888 | tf_op jit(solution)/shard_map/all_to_all | solution.py:62
  9.9 1.1 multiply_convert_fusion
  11.1 0.2 pad_maximum_fusion.23
  11.3 4.7 %collective-permute-start = (bf16[2,8,4,1,512]{4,3,2,1,0:T(2,128)(2,1)S(1)}, bf16[2,8,4,1,512]{4,3,2,1,0:T(2,128)(2,1)S(1)}, u32[]{:S(2)}, u32[]{:S(2)}) collective-permute-start(bf16[2,8,4,1,512]{4,3,2,1,0:T(2,128)(2,1)S(1)} %get-tuple-element.211), channel_id=1, source_target_pairs={{0,16},{16,32},{32,48},{48,64},{64,80},{80,96},{96,112},{112,128},... | collective-permute-start | bytes 196616 | tf_op jit(solution)/shard_map/ppermute | solution.py:14
  16.0 1.9 collective-permute-start.1
  17.9 4.7 %collective-permute-done.1 = bf16[2,8,4,1,512]{4,3,2,1,0:T(2,128)(2,1)S(1)} collective-permute-done((bf16[2,8,4,1,512]{4,3,2,1,0:T(2,128)(2,1)S(1)}, bf16[2,8,4,1,512]{4,3,2,1,0:T(2,128)(2,1)S(1)}, u32[]{:S(2)}, u32[]{:S(2)}) %collective-permute-start.1) | collective-permute-done | bytes 65568 | tf_op jit(solution)/shard_map/ppermute | solution.py:15
  22.7 0.3 pad_maximum_fusion.15
  23.0 3.6 %collective-permute-start.2 = (bf16[2,8,1,10,512]{4,3,2,1,0:T(8,128)(2,1)S(1)}, bf16[2,8,1,10,512]{4,3,2,1,0:T(8,128)(2,1)S(1)}, u32[]{:S(2)}, u32[]{:S(2)}) collective-permute-start(bf16[2,8,1,10,512]{4,3,2,1,0:T(8,128)(2,1)S(1)} %get-tuple-element.203), channel_id=1, source_target_pairs={{0,1},{1,2},{2,3},{4,5},{5,6},{6,7},{8,9},{9,10},{10,11},{12,13},{... | collective-permute-start | bytes 491528 | tf_op jit(solution)/shard_map/ppermute | solution.py:14
  26.5 1.3 collective-permute-start.3
  27.8 23.2 %collective-permute-done.2 = bf16[2,8,1,10,512]{4,3,2,1,0:T(8,128)(2,1)S(1)} collective-permute-done((bf16[2,8,1,10,512]{4,3,2,1,0:T(8,128)(2,1)S(1)}, bf16[2,8,1,10,512]{4,3,2,1,0:T(8,128)(2,1)S(1)}, u32[]{:S(2)}, u32[]{:S(2)}) %collective-permute-start.2) | collective-permute-done | bytes 163872 | tf_op jit(solution)/shard_map/ppermute | solution.py:14
  51.0 2.7 %collective-permute-done.3 = bf16[2,8,1,10,512]{4,3,2,1,0:T(8,128)(2,1)S(1)} collective-permute-done((bf16[2,8,1,10,512]{4,3,2,1,0:T(8,128)(2,1)S(1)}, bf16[2,8,1,10,512]{4,3,2,1,0:T(8,128)(2,1)S(1)}, u32[]{:S(2)}, u32[]{:S(2)}) %collective-permute-start.3) | collective-permute-done | bytes 163872 | tf_op jit(solution)/shard_map/ppermute | solution.py:15
  53.8 0.7 maximum_convert_fusion
  54.5 1.8 fusion.314
  56.3 2.1 fusion.287
  58.4 7.9 %fusion.40 = f32[2,8,4,8,512]{4,3,2,1,0:T(8,128)} fusion(f32[2,8,6,10,512]{4,3,2,1,0:T(8,128)S(1)} %maximum_convert_fusion, f32[4,8,512]{2,1,0:T(8,128)} %get-tuple-element.148, f32[4,8,512]{2,1,0:T(8,128)} %get-tuple-element.149, f32[4,8,512]{2,1,0:T(8,128)} %get-tuple-element.150, f32[4,8,512]{2,1,0:T(8,128)} %get-tuple-element.151, ...), kind=kLoop, calls=%fused_computation.119 | loop fusion | flops 13893632 | bytes 15400960 | tf_op jit(solution)/shard_map/add | solution.py:28
  66.3 2.9 %convert_bitcast_fusion.4 = (bf16[1,8,4,8,512]{4,3,2,1,0:T(8,128)(2,1)S(1)}, f32[8,4,8,512]{3,2,1,0:T(8,128)}, bf16[1,8,4,8,512]{4,3,2,1,0:T(8,128)(2,1)S(1)}, f32[8,4,8,512]{3,2,1,0:T(8,128)}) fusion(f32[4,8,4,8,512]{4,3,2,1,0:T(8,128)} %param.17, f32[8,4,8,512]{3,2,1,0:T(8,128)} %param.12, f32[8]{0:T(128)S(1)} %copy-done.9, ...), kind=kLoop, calls=%fused_computation.373 | loop fusion | flops 2490368 | bytes 3735584 | tf_op jit(solution)/shard_map/stack | solution.py:67
  69.2 0.2 pad_maximum_fusion.21
  69.4 6.8 %collective-permute-start.4 = (bf16[2,8,4,1,512]{4,3,2,1,0:T(2,128)(2,1)S(1)}, bf16[2,8,4,1,512]{4,3,2,1,0:T(2,128)(2,1)S(1)}, u32[]{:S(2)}, u32[]{:S(2)}) collective-permute-start(bf16[2,8,4,1,512]{4,3,2,1,0:T(2,128)(2,1)S(1)} %get-tuple-element.209), channel_id=1, source_target_pairs={{0,16},{16,32},{32,48},{48,64},{64,80},{80,96},{96,112},{112,128},... | collective-permute-start | bytes 196616 | tf_op jit(solution)/shard_map/ppermute | solution.py:14
  76.2 1.9 collective-permute-start.5
  78.1 2.1 fusion.315
  80.3 2.2 collective-permute-done.5
  82.5 0.3 pad_maximum_fusion.11
  82.8 3.1 %collective-permute-start.6 = (bf16[2,8,1,10,512]{4,3,2,1,0:T(8,128)(2,1)S(1)}, bf16[2,8,1,10,512]{4,3,2,1,0:T(8,128)(2,1)S(1)}, u32[]{:S(2)}, u32[]{:S(2)}) collective-permute-start(bf16[2,8,1,10,512]{4,3,2,1,0:T(8,128)(2,1)S(1)} %get-tuple-element.201), channel_id=1, source_target_pairs={{0,1},{1,2},{2,3},{4,5},{5,6},{6,7},{8,9},{9,10},{10,11},{12,13},{... | collective-permute-start | bytes 491528 | tf_op jit(solution)/shard_map/ppermute | solution.py:14
  85.9 1.3 collective-permute-start.7
  87.2 2.0 fusion.316
  89.4 4.1 %collective-permute-done.7 = bf16[2,8,1,10,512]{4,3,2,1,0:T(8,128)(2,1)S(1)} collective-permute-done((bf16[2,8,1,10,512]{4,3,2,1,0:T(8,128)(2,1)S(1)}, bf16[2,8,1,10,512]{4,3,2,1,0:T(8,128)(2,1)S(1)}, u32[]{:S(2)}, u32[]{:S(2)}) %collective-permute-start.7) | collective-permute-done | bytes 163872 | tf_op jit(solution)/shard_map/ppermute | solution.py:15
  93.5 0.7 maximum_convert_fusion.1
  94.3 8.0 %fusion.84 = f32[2,8,4,8,512]{4,3,2,1,0:T(8,128)} fusion(f32[2,8,6,10,512]{4,3,2,1,0:T(8,128)S(1)} %maximum_convert_fusion.1, f32[4,8,512]{2,1,0:T(8,128)} %get-tuple-element.121, f32[4,8,512]{2,1,0:T(8,128)} %get-tuple-element.122, f32[4,8,512]{2,1,0:T(8,128)} %get-tuple-element.123, f32[4,8,512]{2,1,0:T(8,128)} %get-tuple-element.125, ...), kind=kLoop, calls=%fused_computation.163 | loop fusion | flops 13893632 | bytes 15400960 | tf_op jit(solution)/shard_map/add | solution.py:28
  102.2 2.9 %convert_bitcast_fusion.2 = (bf16[1,8,4,8,512]{4,3,2,1,0:T(8,128)(2,1)S(1)}, f32[8,4,8,512]{3,2,1,0:T(8,128)}, bf16[1,8,4,8,512]{4,3,2,1,0:T(8,128)(2,1)S(1)}, f32[8,4,8,512]{3,2,1,0:T(8,128)}) fusion(f32[8,4,8,512]{3,2,1,0:T(8,128)} %get-tuple-element.66, f32[8,4,8,512]{3,2,1,0:T(8,128)} %get-tuple-element.196, f32[8]{0:T(128)S(1)} %copy-done.9, ...), kind=kLoop, calls=%fused_computation.371 | loop fusion | flops 2228224 | bytes 3735584 | tf_op jit(solution)/shard_map/stack | solution.py:67
  105.1 0.2 pad_maximum_fusion.19
  105.3 4.6 %collective-permute-start.8 = (bf16[2,8,4,1,512]{4,3,2,1,0:T(2,128)(2,1)S(1)}, bf16[2,8,4,1,512]{4,3,2,1,0:T(2,128)(2,1)S(1)}, u32[]{:S(2)}, u32[]{:S(2)}) collective-permute-start(bf16[2,8,4,1,512]{4,3,2,1,0:T(2,128)(2,1)S(1)} %get-tuple-element.207), channel_id=1, source_target_pairs={{0,16},{16,32},{32,48},{48,64},{64,80},{80,96},{96,112},{112,128},... | collective-permute-start | bytes 196616 | tf_op jit(solution)/shard_map/ppermute | solution.py:14
  109.9 2.1 collective-permute-start.9
  112.0 4.2 %collective-permute-done.9 = bf16[2,8,4,1,512]{4,3,2,1,0:T(2,128)(2,1)S(1)} collective-permute-done((bf16[2,8,4,1,512]{4,3,2,1,0:T(2,128)(2,1)S(1)}, bf16[2,8,4,1,512]{4,3,2,1,0:T(2,128)(2,1)S(1)}, u32[]{:S(2)}, u32[]{:S(2)}) %collective-permute-start.9) | collective-permute-done | bytes 65568 | tf_op jit(solution)/shard_map/ppermute | solution.py:15
  116.2 0.3 pad_maximum_fusion.7
  116.5 2.9 %collective-permute-start.10 = (bf16[2,8,1,10,512]{4,3,2,1,0:T(8,128)(2,1)S(1)}, bf16[2,8,1,10,512]{4,3,2,1,0:T(8,128)(2,1)S(1)}, u32[]{:S(2)}, u32[]{:S(2)}) collective-permute-start(bf16[2,8,1,10,512]{4,3,2,1,0:T(8,128)(2,1)S(1)} %get-tuple-element.199), channel_id=1, source_target_pairs={{0,1},{1,2},{2,3},{4,5},{5,6},{6,7},{8,9},{9,10},{10,11},{12,13},{... | collective-permute-start | bytes 491528 | tf_op jit(solution)/shard_map/ppermute | solution.py:14
  119.4 1.3 collective-permute-start.11
  120.7 2.1 fusion.235
  122.9 4.1 %collective-permute-done.11 = bf16[2,8,1,10,512]{4,3,2,1,0:T(8,128)(2,1)S(1)} collective-permute-done((bf16[2,8,1,10,512]{4,3,2,1,0:T(8,128)(2,1)S(1)}, bf16[2,8,1,10,512]{4,3,2,1,0:T(8,128)(2,1)S(1)}, u32[]{:S(2)}, u32[]{:S(2)}) %collective-permute-start.11) | collective-permute-done | bytes 163872 | tf_op jit(solution)/shard_map/ppermute | solution.py:15
  127.0 0.7 maximum_convert_fusion.2
  127.8 7.9 %fusion.128 = f32[2,8,4,8,512]{4,3,2,1,0:T(8,128)} fusion(f32[2,8,6,10,512]{4,3,2,1,0:T(8,128)S(1)} %maximum_convert_fusion.2, f32[4,8,512]{2,1,0:T(8,128)} %get-tuple-element.94, f32[4,8,512]{2,1,0:T(8,128)} %get-tuple-element.95, f32[4,8,512]{2,1,0:T(8,128)} %get-tuple-element.96, f32[4,8,512]{2,1,0:T(8,128)} %get-tuple-element.97, ...), kind=kLoop, calls=%fused_computation.207 | loop fusion | flops 13893632 | bytes 15400960 | tf_op jit(solution)/shard_map/add | solution.py:28
  135.7 2.9 %convert_bitcast_fusion = (bf16[1,8,4,8,512]{4,3,2,1,0:T(8,128)(2,1)S(1)}, f32[8,4,8,512]{3,2,1,0:T(8,128)}, bf16[1,8,4,8,512]{4,3,2,1,0:T(8,128)(2,1)S(1)}, f32[8,4,8,512]{3,2,1,0:T(8,128)}) fusion(f32[8,4,8,512]{3,2,1,0:T(8,128)} %get-tuple-element.62, f32[8,4,8,512]{3,2,1,0:T(8,128)} %get-tuple-element.194, f32[8]{0:T(128)S(1)} %copy-done.9, ...), kind=kLoop, calls=%fused_computation.369 | loop fusion | flops 2228224 | bytes 3735584 | tf_op jit(solution)/shard_map/stack | solution.py:67
  138.6 0.2 pad_maximum_fusion.17
  138.7 4.6 %collective-permute-start.12 = (bf16[2,8,4,1,512]{4,3,2,1,0:T(2,128)(2,1)S(1)}, bf16[2,8,4,1,512]{4,3,2,1,0:T(2,128)(2,1)S(1)}, u32[]{:S(2)}, u32[]{:S(2)}) collective-permute-start(bf16[2,8,4,1,512]{4,3,2,1,0:T(2,128)(2,1)S(1)} %get-tuple-element.205), channel_id=1, source_target_pairs={{0,16},{16,32},{32,48},{48,64},{64,80},{80,96},{96,112},{112,128},... | collective-permute-start | bytes 196616 | tf_op jit(solution)/shard_map/ppermute | solution.py:14
  143.3 1.9 collective-permute-start.13
  145.3 0.7 compare_reduce_fusion.1
  146.0 3.7 %collective-permute-done.13 = bf16[2,8,4,1,512]{4,3,2,1,0:T(2,128)(2,1)S(1)} collective-permute-done((bf16[2,8,4,1,512]{4,3,2,1,0:T(2,128)(2,1)S(1)}, bf16[2,8,4,1,512]{4,3,2,1,0:T(2,128)(2,1)S(1)}, u32[]{:S(2)}, u32[]{:S(2)}) %collective-permute-start.13) | collective-permute-done | bytes 65568 | tf_op jit(solution)/shard_map/ppermute | solution.py:15
  149.6 0.3 pad_maximum_fusion.3
  149.9 2.4 collective-permute-start.14
  152.3 1.4 collective-permute-start.15
  153.8 2.1 fusion.317
  155.9 4.2 %collective-permute-done.15 = bf16[2,8,1,10,512]{4,3,2,1,0:T(8,128)(2,1)S(1)} collective-permute-done((bf16[2,8,1,10,512]{4,3,2,1,0:T(8,128)(2,1)S(1)}, bf16[2,8,1,10,512]{4,3,2,1,0:T(8,128)(2,1)S(1)}, u32[]{:S(2)}, u32[]{:S(2)}) %collective-permute-start.15) | collective-permute-done | bytes 163872 | tf_op jit(solution)/shard_map/ppermute | solution.py:15
  160.1 0.7 maximum_convert_fusion.3
  160.9 7.9 %fusion.172 = f32[2,8,4,8,512]{4,3,2,1,0:T(8,128)} fusion(f32[2,8,6,10,512]{4,3,2,1,0:T(8,128)S(1)} %maximum_convert_fusion.3, f32[4,8,512]{2,1,0:T(8,128)} %get-tuple-element.68, f32[4,8,512]{2,1,0:T(8,128)} %get-tuple-element.69, f32[4,8,512]{2,1,0:T(8,128)} %get-tuple-element.70, f32[4,8,512]{2,1,0:T(8,128)} %get-tuple-element.71, ...), kind=kLoop, calls=%fused_computation.251 | loop fusion | flops 13893632 | bytes 15400960 | tf_op jit(solution)/shard_map/add | solution.py:28
  168.8 4.9 %fusion.200 = (f32[]{:T(128)}, f32[]{:T(128)}, f32[]{:T(128)}, f32[]{:T(128)}, f32[]{:T(128)}, /*index=5*/f32[]{:T(128)}, f32[]{:T(128)}, f32[]{:T(128)}, f32[]{...) fusion(f32[4,8,4,8,512]{4,3,2,1,0:T(8,128)} %param.17, ...), kind=kLoop, calls=%fused_computation.332 | loop fusion | flops 6422512 | bytes 5832800 | tf_op jit(solution)/shard_map/reduce_sum | solution.py:91
  173.7 10.0 %stack.131 = f32[16]{0:T(128)S(1)} concatenate(f32[1]{0:T(128)} %bitcast.135, f32[1]{0:T(128)} %bitcast.137, f32[1]{0:T(128)} %bitcast.139, f32[1]{0:T(128)} %bitcast.140, f32[1]{0:T(128)} %bitcast.141, f32[1]{0:T(128)} %bitcast.142, f32[1]{0:T(128)} %bitcast.143, f32[1]{0:T(128)} %bitcast.144, f32[1]{0:T(128)} %bitcast.145, f32[1]{0:T(128)} %bitcast.146, f32[1]{0:T(128)} %bitcast.147, ...), dimensions={0} | concatenate | bytes 128 | tf_op jit(solution)/shard_map/stack | solution.py:92
  183.7 0.6 broadcast_select_fusion
  184.4 10.4 %all_to_all.35 = f32[16,1,128]{2,1,0:T(1,128)S(1)} all-to-all(f32[16,1,128]{2,1,0:T(1,128)S(1)} %broadcast_in_dim.23), channel_id=1, replica_groups=mesh['space'=16,'tracer'=4,'month'=4] {'tracer','month'}, dimensions={0} | all-to-all | bytes 16384 | tf_op jit(solution)/shard_map/all_to_all | solution.py:43
  194.8 20.6 %all_to_all.36 = f32[16,1,128]{2,1,0:T(1,128)S(1)} all-to-all(f32[16,1,128]{2,1,0:T(1,128)S(1)} %broadcast_in_dim.24), channel_id=1, replica_groups=mesh['space'=16,'tracer'=4,'month'=4] {'space'}, dimensions={0} | all-to-all | bytes 16384 | tf_op jit(solution)/shard_map/all_to_all | solution.py:43
  215.5 0.6 multiply_reduce_fusion.4
  216.1 0.7 fusion.326
  236.4 0.3 multiply_reduce_fusion.1
  236.9 0.9 broadcast_divide_fusion
  237.8 0.6 pad_maximum_fusion.24
  (41 shorter events, 0.7 us)
Async XLA Ops:
  4.7 5.1 %copy-start.7 = (s32[8,512]{1,0:T(8,128)S(1)}, s32[8,512]{1,0:T(8,128)}, u32[]{:S(2)}) copy-start(s32[8,512]{1,0:T(8,128)} %param.15) | copy-start | bytes 49156
  4.7 5.2 %copy-start.8 = (s32[8,512]{1,0:T(8,128)S(1)}, s32[8,512]{1,0:T(8,128)}, u32[]{:S(2)}) copy-start(s32[8,512]{1,0:T(8,128)} %param.16) | copy-start | bytes 49156
  4.7 6.4 %copy-start.1 = (f32[8,4,8,512]{3,2,1,0:T(8,128)S(1)}, f32[8,4,8,512]{3,2,1,0:T(8,128)}, u32[]{:S(2)}) copy-start(f32[8,4,8,512]{3,2,1,0:T(8,128)} %param.12) | copy-start | bytes 1572868
  4.7 49.8 %all-to-all-start.2 = ((bf16[1,27,16,8,512]{4,3,1,0,2:T(8,128)(2,1)}), bf16[1,27,16,8,512]{4,3,1,0,2:T(8,128)(2,1)}, u32[]{:S(2)}, u32[]{:S(2)}) async-start(bf16[1,27,16,8,512]{4,3,1,0,2:T(8,128)(2,1)} %copy.14), calls=%async_computation.2 | async-start | bytes 7077888 | tf_op jit(solution)/shard_map/all_to_all | solution.py:62
  11.3 6.6 %collective-permute-start = (bf16[2,8,4,1,512]{4,3,2,1,0:T(2,128)(2,1)S(1)}, bf16[2,8,4,1,512]{4,3,2,1,0:T(2,128)(2,1)S(1)}, u32[]{:S(2)}, u32[]{:S(2)}) collective-permute-start(bf16[2,8,4,1,512]{4,3,2,1,0:T(2,128)(2,1)S(1)} %get-tuple-element.211), channel_id=1, source_target_pairs={{0,16},{16,32},{32,48},{48,64},{64,80},{80,96},{96,112},{112,128},... | collective-permute-start | bytes 196616 | tf_op jit(solution)/shard_map/ppermute | solution.py:14
  16.0 6.7 %collective-permute-start.1 = (bf16[2,8,4,1,512]{4,3,2,1,0:T(2,128)(2,1)S(1)}, bf16[2,8,4,1,512]{4,3,2,1,0:T(2,128)(2,1)S(1)}, u32[]{:S(2)}, u32[]{:S(2)}) collective-permute-start(bf16[2,8,4,1,512]{4,3,2,1,0:T(2,128)(2,1)S(1)} %get-tuple-element.212), channel_id=1, source_target_pairs={{16,0},{32,16},{48,32},{64,48},{80,64},{96,80},{112,96},{128,112},... | collective-permute-start | bytes 196616 | tf_op jit(solution)/shard_map/ppermute | solution.py:15
  23.0 28.1 %collective-permute-start.2 = (bf16[2,8,1,10,512]{4,3,2,1,0:T(8,128)(2,1)S(1)}, bf16[2,8,1,10,512]{4,3,2,1,0:T(8,128)(2,1)S(1)}, u32[]{:S(2)}, u32[]{:S(2)}) collective-permute-start(bf16[2,8,1,10,512]{4,3,2,1,0:T(8,128)(2,1)S(1)} %get-tuple-element.203), channel_id=1, source_target_pairs={{0,1},{1,2},{2,3},{4,5},{5,6},{6,7},{8,9},{9,10},{10,11},{12,13},{... | collective-permute-start | bytes 491528 | tf_op jit(solution)/shard_map/ppermute | solution.py:14
  26.5 27.2 %collective-permute-start.3 = (bf16[2,8,1,10,512]{4,3,2,1,0:T(8,128)(2,1)S(1)}, bf16[2,8,1,10,512]{4,3,2,1,0:T(8,128)(2,1)S(1)}, u32[]{:S(2)}, u32[]{:S(2)}) collective-permute-start(bf16[2,8,1,10,512]{4,3,2,1,0:T(8,128)(2,1)S(1)} %get-tuple-element.204), channel_id=1, source_target_pairs={{1,0},{2,1},{3,2},{5,4},{6,5},{7,6},{9,8},{10,9},{11,10},{13,12},{... | collective-permute-start | bytes 491528 | tf_op jit(solution)/shard_map/ppermute | solution.py:15
  58.4 7.9 %copy-start.9 = (f32[8]{0:T(128)S(1)}, f32[8]{0:T(128)}, u32[]{:S(2)}) copy-start(f32[8]{0:T(128)} %param.14) | copy-start | bytes 100
  69.4 10.9 %collective-permute-start.4 = (bf16[2,8,4,1,512]{4,3,2,1,0:T(2,128)(2,1)S(1)}, bf16[2,8,4,1,512]{4,3,2,1,0:T(2,128)(2,1)S(1)}, u32[]{:S(2)}, u32[]{:S(2)}) collective-permute-start(bf16[2,8,4,1,512]{4,3,2,1,0:T(2,128)(2,1)S(1)} %get-tuple-element.209), channel_id=1, source_target_pairs={{0,16},{16,32},{32,48},{48,64},{64,80},{80,96},{96,112},{112,128},... | collective-permute-start | bytes 196616 | tf_op jit(solution)/shard_map/ppermute | solution.py:14
  76.2 6.3 %collective-permute-start.5 = (bf16[2,8,4,1,512]{4,3,2,1,0:T(2,128)(2,1)S(1)}, bf16[2,8,4,1,512]{4,3,2,1,0:T(2,128)(2,1)S(1)}, u32[]{:S(2)}, u32[]{:S(2)}) collective-permute-start(bf16[2,8,4,1,512]{4,3,2,1,0:T(2,128)(2,1)S(1)} %get-tuple-element.210), channel_id=1, source_target_pairs={{16,0},{32,16},{48,32},{64,48},{80,64},{96,80},{112,96},{128,112},... | collective-permute-start | bytes 196616 | tf_op jit(solution)/shard_map/ppermute | solution.py:15
  82.8 6.6 %collective-permute-start.6 = (bf16[2,8,1,10,512]{4,3,2,1,0:T(8,128)(2,1)S(1)}, bf16[2,8,1,10,512]{4,3,2,1,0:T(8,128)(2,1)S(1)}, u32[]{:S(2)}, u32[]{:S(2)}) collective-permute-start(bf16[2,8,1,10,512]{4,3,2,1,0:T(8,128)(2,1)S(1)} %get-tuple-element.201), channel_id=1, source_target_pairs={{0,1},{1,2},{2,3},{4,5},{5,6},{6,7},{8,9},{9,10},{10,11},{12,13},{... | collective-permute-start | bytes 491528 | tf_op jit(solution)/shard_map/ppermute | solution.py:14
  85.9 7.6 %collective-permute-start.7 = (bf16[2,8,1,10,512]{4,3,2,1,0:T(8,128)(2,1)S(1)}, bf16[2,8,1,10,512]{4,3,2,1,0:T(8,128)(2,1)S(1)}, u32[]{:S(2)}, u32[]{:S(2)}) collective-permute-start(bf16[2,8,1,10,512]{4,3,2,1,0:T(8,128)(2,1)S(1)} %get-tuple-element.202), channel_id=1, source_target_pairs={{1,0},{2,1},{3,2},{5,4},{6,5},{7,6},{9,8},{10,9},{11,10},{13,12},{... | collective-permute-start | bytes 491528 | tf_op jit(solution)/shard_map/ppermute | solution.py:15
  105.3 6.7 %collective-permute-start.8 = (bf16[2,8,4,1,512]{4,3,2,1,0:T(2,128)(2,1)S(1)}, bf16[2,8,4,1,512]{4,3,2,1,0:T(2,128)(2,1)S(1)}, u32[]{:S(2)}, u32[]{:S(2)}) collective-permute-start(bf16[2,8,4,1,512]{4,3,2,1,0:T(2,128)(2,1)S(1)} %get-tuple-element.207), channel_id=1, source_target_pairs={{0,16},{16,32},{32,48},{48,64},{64,80},{80,96},{96,112},{112,128},... | collective-permute-start | bytes 196616 | tf_op jit(solution)/shard_map/ppermute | solution.py:14
  109.9 6.3 %collective-permute-start.9 = (bf16[2,8,4,1,512]{4,3,2,1,0:T(2,128)(2,1)S(1)}, bf16[2,8,4,1,512]{4,3,2,1,0:T(2,128)(2,1)S(1)}, u32[]{:S(2)}, u32[]{:S(2)}) collective-permute-start(bf16[2,8,4,1,512]{4,3,2,1,0:T(2,128)(2,1)S(1)} %get-tuple-element.208), channel_id=1, source_target_pairs={{16,0},{32,16},{48,32},{64,48},{80,64},{96,80},{112,96},{128,112},... | collective-permute-start | bytes 196616 | tf_op jit(solution)/shard_map/ppermute | solution.py:15
  116.5 6.5 %collective-permute-start.10 = (bf16[2,8,1,10,512]{4,3,2,1,0:T(8,128)(2,1)S(1)}, bf16[2,8,1,10,512]{4,3,2,1,0:T(8,128)(2,1)S(1)}, u32[]{:S(2)}, u32[]{:S(2)}) collective-permute-start(bf16[2,8,1,10,512]{4,3,2,1,0:T(8,128)(2,1)S(1)} %get-tuple-element.199), channel_id=1, source_target_pairs={{0,1},{1,2},{2,3},{4,5},{5,6},{6,7},{8,9},{9,10},{10,11},{12,13},{... | collective-permute-start | bytes 491528 | tf_op jit(solution)/shard_map/ppermute | solution.py:14
  119.4 7.6 %collective-permute-start.11 = (bf16[2,8,1,10,512]{4,3,2,1,0:T(8,128)(2,1)S(1)}, bf16[2,8,1,10,512]{4,3,2,1,0:T(8,128)(2,1)S(1)}, u32[]{:S(2)}, u32[]{:S(2)}) collective-permute-start(bf16[2,8,1,10,512]{4,3,2,1,0:T(8,128)(2,1)S(1)} %get-tuple-element.200), channel_id=1, source_target_pairs={{1,0},{2,1},{3,2},{5,4},{6,5},{7,6},{9,8},{10,9},{11,10},{13,12},{... | collective-permute-start | bytes 491528 | tf_op jit(solution)/shard_map/ppermute | solution.py:15
  138.7 7.2 %collective-permute-start.12 = (bf16[2,8,4,1,512]{4,3,2,1,0:T(2,128)(2,1)S(1)}, bf16[2,8,4,1,512]{4,3,2,1,0:T(2,128)(2,1)S(1)}, u32[]{:S(2)}, u32[]{:S(2)}) collective-permute-start(bf16[2,8,4,1,512]{4,3,2,1,0:T(2,128)(2,1)S(1)} %get-tuple-element.205), channel_id=1, source_target_pairs={{0,16},{16,32},{32,48},{48,64},{64,80},{80,96},{96,112},{112,128},... | collective-permute-start | bytes 196616 | tf_op jit(solution)/shard_map/ppermute | solution.py:14
  143.3 6.3 %collective-permute-start.13 = (bf16[2,8,4,1,512]{4,3,2,1,0:T(2,128)(2,1)S(1)}, bf16[2,8,4,1,512]{4,3,2,1,0:T(2,128)(2,1)S(1)}, u32[]{:S(2)}, u32[]{:S(2)}) collective-permute-start(bf16[2,8,4,1,512]{4,3,2,1,0:T(2,128)(2,1)S(1)} %get-tuple-element.206), channel_id=1, source_target_pairs={{16,0},{32,16},{48,32},{64,48},{80,64},{96,80},{112,96},{128,112},... | collective-permute-start | bytes 196616 | tf_op jit(solution)/shard_map/ppermute | solution.py:15
  149.9 6.0 %collective-permute-start.14 = (bf16[2,8,1,10,512]{4,3,2,1,0:T(8,128)(2,1)S(1)}, bf16[2,8,1,10,512]{4,3,2,1,0:T(8,128)(2,1)S(1)}, u32[]{:S(2)}, u32[]{:S(2)}) collective-permute-start(bf16[2,8,1,10,512]{4,3,2,1,0:T(8,128)(2,1)S(1)} %get-tuple-element.197), channel_id=1, source_target_pairs={{0,1},{1,2},{2,3},{4,5},{5,6},{6,7},{8,9},{9,10},{10,11},{12,13},{... | collective-permute-start | bytes 491528 | tf_op jit(solution)/shard_map/ppermute | solution.py:14
  152.3 8.5 %copy-start.2 = (f32[4,8,512]{2,1,0:T(8,128)S(1)}, f32[4,8,512]{2,1,0:T(8,128)}, u32[]{:S(2)}) copy-start(f32[4,8,512]{2,1,0:T(8,128)} %get-tuple-element.86) | copy-start | bytes 196612
  152.3 8.5 %copy-start.3 = (f32[4,8,512]{2,1,0:T(8,128)S(1)}, f32[4,8,512]{2,1,0:T(8,128)}, u32[]{:S(2)}) copy-start(f32[4,8,512]{2,1,0:T(8,128)} %get-tuple-element.87) | copy-start | bytes 196612
  152.3 8.5 %copy-start.4 = (f32[4,8,512]{2,1,0:T(8,128)S(1)}, f32[4,8,512]{2,1,0:T(8,128)}, u32[]{:S(2)}) copy-start(f32[4,8,512]{2,1,0:T(8,128)} %get-tuple-element.88) | copy-start | bytes 196612
  152.3 8.5 %copy-start.5 = (f32[4,8,512]{2,1,0:T(8,128)S(1)}, f32[4,8,512]{2,1,0:T(8,128)}, u32[]{:S(2)}) copy-start(f32[4,8,512]{2,1,0:T(8,128)} %get-tuple-element.89) | copy-start | bytes 196612
  152.3 8.5 %copy-start.6 = (f32[4,8,512]{2,1,0:T(8,128)S(1)}, f32[4,8,512]{2,1,0:T(8,128)}, u32[]{:S(2)}) copy-start(f32[4,8,512]{2,1,0:T(8,128)} %get-tuple-element.90) | copy-start | bytes 196612
  152.3 7.8 %collective-permute-start.15 = (bf16[2,8,1,10,512]{4,3,2,1,0:T(8,128)(2,1)S(1)}, bf16[2,8,1,10,512]{4,3,2,1,0:T(8,128)(2,1)S(1)}, u32[]{:S(2)}, u32[]{:S(2)}) collective-permute-start(bf16[2,8,1,10,512]{4,3,2,1,0:T(8,128)(2,1)S(1)} %get-tuple-element.198), channel_id=1, source_target_pairs={{1,0},{2,1},{3,2},{5,4},{6,5},{7,6},{9,8},{10,9},{11,10},{13,12},{... | collective-permute-start | bytes 491528 | tf_op jit(solution)/shard_map/ppermute | solution.py:15
  168.8 67.6 %copy-start = (f32[4,8,4,8,512]{4,3,2,1,0:T(8,128)S(1)}, f32[4,8,4,8,512]{4,3,2,1,0:T(8,128)}, u32[]{:S(2)}) copy-start(f32[4,8,4,8,512]{4,3,2,1,0:T(8,128)} %param.17) | copy-start | bytes 6291460
